TPU v7x, 32 devices: a whole 2x2x4 slice. The times are simulated.
32 devices in a mesh: rows: 8 (over z, core), tiles: 4 (over y, x).
Axes of the slice: x: 2, y: 2, z: 4, core: 2. Of those that a mesh axis runs over, the one named last changes fastest.
Arguments:
- features: bfloat16 [4096, 16384], P(('rows', 'tiles')), as said below
- row_salt: int32 [4096], P(('rows', 'tiles')), may hold values from 0 to 32767
- column_multiplier: int32 [16384], replicated, may hold values from 1 to 32767
- column_offset: int32 [16384], replicated, may hold values from 0 to 65520
- thresholds: int32 [16384], replicated, may hold values from 16000 to 65520
Outputs:
- similarity: float32 [256, 16384], P('rows', 'tiles')
Inputs may be any that keep to these rules, and one draw needn't show every extreme that they name: `features`: Real-valued entries of order one.
All inputs are finite; a program needn't handle non-finite values.
Results may differ from a plain program's by a relative error of at most 0.0028.
Values sent between devices are 32-bit elements; how exact they have to be, the bound alone decides.
A program may use at most 64 MiB of HBM per device.

v0:
```python
import jax
import jax.numpy as jnp
from jax import lax
from jax.sharding import PartitionSpec as P

N = 16384
WIN = 256


def sample_block(block, salts, column_multiplier, column_offset, thresholds):
    hashed = (salts[:, None] * column_multiplier[None, :] + column_offset[None, :]) % 65521
    weight = lax.rsqrt(thresholds.astype(jnp.float32) / 65521.0)
    values = block.astype(jnp.float32) * weight[None, :]
    return jnp.where(hashed < thresholds[None, :], values, jnp.zeros_like(values)).astype(
        jnp.bfloat16
    )


def inner_product(left, right):
    return lax.dot_general(
        left, right, (((0,), (0,)), ((), ())), preferred_element_type=jnp.float32
    )


def shards(features, row_salt, column_multiplier, column_offset, thresholds):
    wide = features.astype(jnp.float32)
    squares = lax.psum(jnp.sum(wide * wide, axis=0), ("rows", "tiles"))
    norms = jnp.sqrt(squares + 1e-06)
    sampled = sample_block(features, row_salt, column_multiplier, column_offset, thresholds)
    queries = sampled[:, :WIN]
    count_rows = lax.axis_size("rows")
    count_tiles = lax.axis_size("tiles")
    block_rows = WIN // count_rows
    block_cols = N // count_tiles
    partial_value = inner_product(queries, sampled)
    halfway = lax.psum_scatter(partial_value, "tiles", scatter_dimension=1, tiled=True)
    tile = lax.psum_scatter(halfway, "rows", scatter_dimension=0, tiled=True)
    query_norms = lax.dynamic_slice_in_dim(
        norms, lax.axis_index("rows") * block_rows, block_rows, 0
    )
    column_norms = lax.dynamic_slice_in_dim(
        norms, lax.axis_index("tiles") * block_cols, block_cols, 0
    )
    return tile / (query_norms[:, None] * column_norms[None, :])


def solution(mesh):
    placed = (P(("rows", "tiles"), None), P(("rows", "tiles")), P(), P(), P())
    return jax.shard_map(
        shards, mesh=mesh, in_specs=placed, out_specs=P("rows", "tiles"), check_vma=False
    )
```

profile of v0, /device:TPU:0, one launch (start us, length us, event | category | flops | bytes accessed | tf_op | source)
XLA Modules:
  0.0 245.5 jit_solution(1618224861872326387)
XLA Ops:
  7.4 0.0 reduce-scatter.3.cloned.1.call-start
  7.4 0.9 multiply_rsqrt_fusion
  8.2 9.9 %fusion.2 = (f32[16384]{0:T(1024)}, bf16[128,16384]{1,0:T(8,128)(2,1)S(1)}) fusion(bf16[128,16384]{1,0:T(8,128)(2,1)} %param.5, f32[16384]{0:T(1024)S(1)} %multiply_rsqrt_fusion, s32[16384]{0:T(1024)} %param.9, s32[16384]{0:T(1024)} %param.8, s32[16384]{0:T(1024)} %param.7, s32[128]{0:T(128)} %param.6), kind=kLoop, calls=%fused_computation.5 | loop fusion | flops 31440896 | bytes 8716800 | tf_op jit(solution)/shard_map/reduce_sum | solution.py:27
  18.1 8.1 %fusion.7 = f32[256,16384]{1,0:T(8,128)} fusion(bf16[128,16384]{1,0:T(8,128)(2,1)S(1)} %get-tuple-element.6), kind=kOutput, calls=%fused_computation.12 | convolution fusion | flops 1073741824 | bytes 21037056 | tf_op jit(solution)/shard_map/dot_general | solution.py:20
  26.2 0.0 reduce-scatter.3.cloned.1.call-update
  26.2 0.0 all-reduce.2.cloned.1.call-start
  26.2 0.5 all-reduce.2.cloned.1.call-update
  26.8 0.0 reduce-scatter.5.cloned.1.call-start
  26.8 156.6 %reduce-scatter.3.cloned.1.call-done = f32[256,4096]{1,0:T(8,128)} async-done(((f32[256,16384]{1,0:T(8,128)}), f32[256,4096]{1,0:T(8,128)}) %reduce-scatter.3.cloned.1.call-update) | async-done | bytes 4194320 | tf_op jit(solution)/shard_map/reduce_scatter | solution.py:36
  183.4 0.0 reduce-scatter.5.cloned.1.call-update
  183.4 24.9 %all-reduce.2.cloned.1.call-done = f32[16384]{0:T(1024)} async-done(((f32[16384]{0:T(1024)}), f32[16384]{0:T(1024)}) %all-reduce.2.cloned.1.call-update) | async-done | bytes 65552 | tf_op jit(solution)/shard_map/psum | solution.py:27
  208.3 0.9 add_sqrt_fusion
  209.1 0.1 dynamic_slice.6
  209.2 26.8 %reduce-scatter.5.cloned.1.call-done = f32[32,4096]{1,0:T(8,128)} async-done(((f32[256,4096]{1,0:T(8,128)}), f32[32,4096]{1,0:T(8,128)}) %reduce-scatter.5.cloned.1.call-update) | async-done | bytes 524304 | tf_op jit(solution)/shard_map/reduce_scatter | solution.py:37
  236.1 2.0 multiply_divide_fusion
  (1 shorter events, 0.0 us)
Async XLA Ops:
  7.4 176.0 %reduce-scatter.3.cloned.1.call-start = ((), (), s32[]{:S(2)}) async-start(), calls=%async_computation.2 | async-start | bytes 20971520 | tf_op jit(solution)/shard_map/reduce_scatter | solution.py:36
  26.2 182.1 %all-reduce.2.cloned.1.call-start = ((), (), s32[]{:S(2)}) async-start(), calls=%async_computation.4 | async-start | bytes 131072 | tf_op jit(solution)/shard_map/psum | solution.py:27
  26.8 209.3 %reduce-scatter.5.cloned.1.call-start = ((), (), s32[]{:S(2)}) async-start(), calls=%async_computation.3 | async-start | bytes 4718592 | tf_op jit(solution)/shard_map/reduce_scatter | solution.py:37
Sparse Core Ops, SparseCore 0:
  26.3 157.0 reduce-scatter.2
  185.7 50.3 reduce-scatter.4
Sparse Core Ops, SparseCore 1:
  32.3 176.0 all-reduce.1
where the time goes:
time: 246 us; the launch traced here: 245 us
  waiting for transfers between devices  209 us (85%)
  between operations  14.9 us (6%)
  other arithmetic  13.6 us (6%)
  matrix products  8.08 us (3%)
    reduce_scatter x1, waiting for transfers between devices, shards(): lax.psum_scatter(partial_value, 'tiles', scatter_dimension=1, tiled=True)  157 us
    reduce_scatter x1, waiting for transfers between devices, shards(): tile = lax.psum_scatter(halfway, 'rows', scatter_dimension=0, tiled=True)  26.8 us
    psum x1, waiting for transfers between devices, shards(): squares = lax.psum(jnp.sum(wide * wide, axis=0), ('rows', 'tiles'))  24.9 us
    reduce_sum x1, other arithmetic, shards(): squares = lax.psum(jnp.sum(wide * wide, axis=0), ('rows', 'tiles'))  9.86 us
    dot_general x1, matrix products, inner_product(): lax.dot_general(left, right, (((0,), (0,)), ((), ())), preferred_element_...  8.08 us
  transfers between devices with their start and end apart: 3, of which 3 were waited for; matrix products, arithmetic and copies ran while one was open for 0% of the time, Pallas kernels for 0%

commit v1 on v0

v1 whole, which is shorter than its diff:
```python
import functools

import jax
import jax.numpy as jnp
from jax import lax
from jax.experimental import pallas as pl
from jax.experimental.pallas import tpu as pltpu
from jax.sharding import PartitionSpec as P

WIN = 256
PRIME = 65521
AHEAD = 2
MESH = pl.DeviceIdType.MESH


class Plan:
    def __init__(self, rows, tiles, users, columns):
        self.rows, self.tiles, self.users, self.columns = rows, tiles, users, columns
        self.outer, self.inner = 2, tiles // 2
        self.tile_cols = columns // tiles
        self.tile_rows = WIN // rows
        self.sub = self.tile_cols // 4
        self.width = min(self.sub, 256)
        self.pieces = self.sub // self.width
        self.group = (2 * self.inner, 2 * self.outer)
        self.adds = (self.outer, self.inner)


def fold(h):
    return (h >> 16) * 15 + (h & 65535)


def kernel(
    plan, feat, salt, mult, offset, thr, out, qn, cn,
    saltc, q_own, q0, q1, qt0, qt1, s0, s1, r0, r1, p0, p1, g0, g1, acc, fin, sq, sqr, sqa, sqf,
    q_send, q_recv, a_send0, a_recv0, a_send1, a_recv1, b_send0, b_recv0, b_send1, b_recv1,
    c_send, c_recv, d_send, d_recv, e_send, e_recv,
):
    R, T, users, width, K = plan.rows, plan.tiles, plan.users, plan.width, plan.pieces
    A, B, CT, sub, RB = plan.outer, plan.inner, plan.tile_cols, plan.sub, plan.tile_rows
    r, t = lax.axis_index("rows"), lax.axis_index("tiles")
    c = lax.rem(r, 2)
    base = r - c
    a, b = t // B, lax.rem(t, B)
    q_in, qt, s, rc, part, got = (q0, q1), (qt0, qt1), (s0, s1), (r0, r1), (p0, p1), (g0, g1)
    a_sem, b_sem = ((a_send0, a_recv0), (a_send1, a_recv1)), ((b_send0, b_recv0), (b_send1, b_recv1))

    def member(p, d):
        own = (b if p == 0 else a) * 2 + c
        other = lax.rem(own + d, plan.group[p])
        return other // 2, lax.rem(other, 2)

    def device(p, d):
        along, core = member(p, d)
        return (base + core, a * B + along if p == 0 else along * B + b)

    def adder(p, e):
        if p == 0:
            return (r, lax.rem(a + e, A) * B + b)
        return (r, a * B + lax.rem(b + e, B))

    def remote(src, dst, send, recv, to):
        return pltpu.make_async_remote_copy(
            src_ref=src, dst_ref=dst, send_sem=send, recv_sem=recv, device_id=to, device_id_type=MESH
        )

    def q_copy(p, d):
        i = d - 1 if p == 0 else plan.group[0] - 1 + d - 1
        return remote(q_own, q_in[p].at[d], q_send.at[i], q_recv.at[i], device(p, d))

    def a_copy(p, k, d):
        return remote(
            s[p].at[k, d - 1], rc[p].at[k, pl.ds(d * users, users)],
            a_sem[p][0].at[k, d - 1], a_sem[p][1].at[k, d - 1], device(p, d),
        )

    def b_copy(p, k, e):
        return remote(
            part[p].at[k, e], got[p].at[k, e - 1], b_sem[p][0].at[k, e - 1], b_sem[p][1].at[k, e - 1], adder(p, e)
        )

    def c_copy(p, k, d):
        other = lax.rem(r + d, R)
        return remote(
            acc.at[p, k, pl.ds(pl.multiple_of(other * RB, RB), RB)], fin.at[p, k, d - 1],
            c_send.at[p, k, d - 1], c_recv.at[p, k, d - 1], (other, t),
        )

    def d_copy(d):
        other = lax.rem(t + d, T)
        return remote(sq.at[other], sqr.at[d - 1], d_send.at[d - 1], d_recv.at[d - 1], (r, other))

    def e_copy(d):
        return remote(sqa, sqf.at[d - 1], e_send.at[d - 1], e_recv.at[d - 1], (lax.rem(r + d, R), t))

    step = min(users, 64)

    def sample(start, size, store):
        cols = pl.ds(pl.multiple_of(start, 128), size)
        by, plus, limit = mult[:, cols], offset[:, cols], thr[:, cols]
        weight = lax.rsqrt(limit.astype(jnp.float32) / float(PRIME))

        def body(i, total):
            rows = pl.ds(pl.multiple_of(i * step, step), step)
            x = feat[rows, cols].astype(jnp.float32)
            h = fold(fold(saltc[rows, :] * by + plus))
            h = jnp.where(h >= PRIME, h - PRIME, h)
            value = x * weight
            store(pl.multiple_of(i * step, step), jnp.where(h < limit, value, jnp.zeros_like(value)))
            return total + jnp.sum((x * x).reshape(step // 8, 8, size), axis=0)

        total = lax.fori_loop(0, users // step, body, jnp.zeros((8, size), jnp.float32))
        return jnp.sum(total, axis=0, keepdims=True)

    def sample_for(p, k, d, store):
        along, core = member(p, d)
        for e in range(plan.adds[p]):
            if p == 0:
                tile = lax.rem(a + e, A) * B + along
            else:
                tile = along * B + lax.rem(b + e, B)
            inside = p * (CT // 2) + core * sub + k * width
            squares = sample(tile * CT + inside, width, functools.partial(store, e))
            sq[tile, :, pl.ds(pl.multiple_of(inside, 128), width)] = squares

    def gather_piece(k):
        for p in range(2):
            def away(d, _):
                def store(e, row, value):
                    s[p][k, d - 1, pl.ds(row, step), pl.ds(e * width, width)] = value

                sample_for(p, k, d, store)
                a_copy(p, k, d).start()
                return 0

            lax.fori_loop(1, plan.group[p], away, 0)
        for p in range(2):
            def store(e, row, value):
                rc[p][k, pl.ds(row, step), pl.ds(e * width, width)] = value

            sample_for(p, k, 0, store)

    barrier = pltpu.get_barrier_semaphore()
    for d in range(1, 2 * T):
        other = lax.rem(t * 2 + c + d, 2 * T)
        pl.semaphore_signal(
            barrier, inc=1, device_id=(base + lax.rem(other, 2), other // 2), device_id_type=MESH
        )
    for d in range(1, R):
        pl.semaphore_signal(barrier, inc=1, device_id=(lax.rem(r + d, R), t), device_id_type=MESH)

    diagonal = lax.broadcasted_iota(jnp.int32, (users, users), 0) == lax.broadcasted_iota(
        jnp.int32, (users, users), 1
    )
    spread = jnp.where(diagonal, jnp.broadcast_to(salt[...].astype(jnp.float32), (users, users)), 0.0)
    saltc[...] = jnp.sum(spread, axis=1, keepdims=True).astype(jnp.int32)

    def store_q(row, value):
        q_own[pl.ds(row, step), :] = value

    q_squares = sample(0, WIN, store_q)
    for tile in range(T):
        sq[tile, :, pl.ds(CT, WIN)] = q_squares
    pl.semaphore_wait(barrier, 2 * T - 1 + R - 1)

    for p in range(2):
        for d in range(1, plan.group[p]):
            q_copy(p, d).start()
    for k in range(min(AHEAD, K)):
        gather_piece(k)
    for p in range(2):
        qt[p][:, pl.ds(0, users)] = q_own[...].T.astype(jnp.bfloat16)
        for d in range(1, plan.group[p]):
            q_copy(p, d).wait()
            qt[p][:, pl.ds(d * users, users)] = q_in[p][d].T.astype(jnp.bfloat16)

    for k in range(K + 1):
        if k < K:
            for p in range(2):
                for d in range(1, plan.group[p]):
                    a_copy(p, k, d).wait_recv()
                for e in list(range(1, plan.adds[p])) + [0]:
                    block = rc[p][k, :, pl.ds(e * width, width)].astype(jnp.bfloat16)
                    part[p][k, e] = jnp.dot(qt[p][...], block, preferred_element_type=jnp.float32)
                    if e:
                        b_copy(p, k, e).start()
        if k + AHEAD < K:
            gather_piece(k + AHEAD)
        if k == max(0, K - 1 - AHEAD):
            for d in range(1, T):
                d_copy(d).start()
        if k >= 1:
            for p in range(2):
                total = part[p][k - 1, 0]
                for e in range(1, plan.adds[p]):
                    b_copy(p, k - 1, e).wait_recv()
                    total = total + got[p][k - 1, e - 1]
                acc[p, k - 1] = total
                for d in range(1, R):
                    c_copy(p, k - 1, d).start()
        if k == K - 1:
            total = sq[t]
            for d in range(1, T):
                d_copy(d).wait_recv()
                total = total + sqr[d - 1]
            sqa[...] = total
            for d in range(1, R):
                e_copy(d).start()

    squares = sqa[...]
    for d in range(1, R):
        e_copy(d).wait_recv()
        squares = squares + sqf[d - 1]
    norms = jnp.sqrt(squares + 1e-06)
    cn[...] = norms[:, :CT]
    mine = lax.broadcasted_iota(jnp.int32, (RB, WIN), 1) == r * RB + lax.broadcasted_iota(
        jnp.int32, (RB, WIN), 0
    )
    qn[...] = jnp.sum(
        jnp.where(mine, jnp.broadcast_to(norms[:, CT:], (RB, WIN)), 0.0), axis=1, keepdims=True
    )

    for k in range(K):
        for p in range(2):
            same = acc[p, k, pl.ds(pl.multiple_of(r * RB, RB), RB)]
            cross = None
            for d in range(1, R):
                c_copy(p, k, d).wait_recv()
                piece = fin[p, k, d - 1]
                if d % 2 == 0:
                    same = same + piece
                else:
                    cross = piece if cross is None else cross + piece
            for core, value in ((c, same), (1 - c, cross)):
                start = pl.multiple_of(p * (CT // 2) + core * sub + k * width, 128)
                out[:, pl.ds(start, width)] = value

    for k in range(K):
        for p in range(2):
            for d in range(1, plan.group[p]):
                a_copy(p, k, d).wait_send()
            for e in range(1, plan.adds[p]):
                b_copy(p, k, e).wait_send()
            for d in range(1, R):
                c_copy(p, k, d).wait_send()
    for d in range(1, T):
        d_copy(d).wait_send()
    for d in range(1, R):
        e_copy(d).wait_send()


def shards(features, row_salt, column_multiplier, column_offset, thresholds):
    users, columns = features.shape
    plan = Plan(lax.axis_size("rows"), lax.axis_size("tiles"), users, columns)
    R, T, K, width, CT, RB = plan.rows, plan.tiles, plan.pieces, plan.width, plan.tile_cols, plan.tile_rows
    f32, vmem = jnp.float32, pltpu.VMEM
    G, U = plan.group, plan.adds

    def pair(make):
        return [make(0), make(1)]

    def sems(*shape):
        return [pltpu.SemaphoreType.DMA(shape)] * 2

    scratch = (
        [vmem((users, 1), jnp.int32), vmem((users, WIN), f32)]
        + pair(lambda p: vmem((G[p], users, WIN), f32))
        + pair(lambda p: vmem((WIN, G[p] * users), jnp.bfloat16))
        + pair(lambda p: vmem((K, G[p] - 1, users, U[p] * width), f32))
        + pair(lambda p: vmem((K, G[p] * users, U[p] * width), f32))
        + pair(lambda p: vmem((K, U[p], WIN, width), f32))
        + pair(lambda p: vmem((K, U[p] - 1, WIN, width), f32))
        + [vmem((2, K, WIN, width), f32), vmem((2, K, R - 1, RB, width), f32)]
        + [vmem((T, 1, CT + WIN), f32), vmem((T - 1, 1, CT + WIN), f32)]
        + [vmem((1, CT + WIN), f32), vmem((R - 1, 1, CT + WIN), f32)]
        + sems(G[0] + G[1] - 2)
        + sems(K, G[0] - 1) + sems(K, G[1] - 1)
        + sems(K, U[0] - 1) + sems(K, U[1] - 1)
        + sems(2, K, R - 1) + sems(T - 1) + sems(R - 1)
    )
    spec = pl.BlockSpec(memory_space=pltpu.VMEM)
    gram, query_norms, column_norms = pl.pallas_call(
        functools.partial(kernel, plan),
        out_shape=(
            jax.ShapeDtypeStruct((RB, CT), f32),
            jax.ShapeDtypeStruct((RB, 1), f32),
            jax.ShapeDtypeStruct((1, CT), f32),
        ),
        in_specs=[spec] * 5,
        out_specs=(spec,) * 3,
        scratch_shapes=scratch,
        compiler_params=pltpu.CompilerParams(
            collective_id=0, has_side_effects=True, vmem_limit_bytes=60 * 1024 * 1024
        ),
        name="similarity",
    )(
        features,
        row_salt.reshape(1, users),
        column_multiplier.reshape(1, columns),
        column_offset.reshape(1, columns),
        thresholds.reshape(1, columns),
    )
    return gram / (query_norms * column_norms)


def solution(mesh):
    placed = (P(("rows", "tiles"), None), P(("rows", "tiles")), P(), P(), P())
    return jax.shard_map(
        shards, mesh=mesh, in_specs=placed, out_specs=P("rows", "tiles"), check_vma=False
    )
```

time: 246 us -> 109 us (0.44)
  waiting for transfers between devices: 209 us -> 0 us
  Pallas kernels: 0 us -> 106 us
  between operations: 14.9 us -> 0.01 us
  other arithmetic: 13.6 us -> 2.82 us
  matrix products: 8.08 us -> 0 us
    reduce_scatter x2 -> x0, waiting for transfers between devices: 183 us -> none  [the longest x1 157 us: shards(): lax.psum_scatter(partial_value, 'tiles', scatter_dimension=1, tiled=True)]
    pallas_call x0 -> x1, Pallas kernels: none -> 106 us  [shards(): pl.pallas_call(functools.partial(kernel, plan), out_shape=(jax.ShapeDtype...]
    psum x1 -> x0, waiting for transfers between devices: 24.9 us -> none  [shards(): squares = lax.psum(jnp.sum(wide * wide, axis=0), ('rows', 'tiles'))]
    reduce_sum x1 -> x0, other arithmetic: 9.86 us -> none  [shards(): squares = lax.psum(jnp.sum(wide * wide, axis=0), ('rows', 'tiles'))]
    dot_general x1 -> x0, matrix products: 8.08 us -> none  [inner_product(): lax.dot_general(left, right, (((0,), (0,)), ((), ())), preferred_element_...]
  transfers between devices with their start and end apart: 3 -> 0, of which waited for: 3 -> 0; matrix products, arithmetic and copies ran while one was open for 0% -> 0% of each run, Pallas kernels for 0% -> 0%
where the time goes in v1:
time: 109 us
  Pallas kernels  106 us (97%)
  other arithmetic  2.82 us (3%)
    pallas_call x1, Pallas kernels, shards(): pl.pallas_call(functools.partial(kernel, plan), out_shape=(jax.ShapeDtype...  106 us

profile of v1, /device:TPU:0, one launch (start us, length us, event | category | flops | bytes accessed | tf_op | source)
XLA Modules:
  0.0 109.0 jit_solution(10618969714619488190)
XLA Ops:
  0.0 106.1 %similarity.1 = (f32[32,4096]{1,0:T(8,128)}, f32[32,1]{1,0:T(8,128)}, f32[1,4096]{1,0:T(1,128)}) custom-call(bf16[128,16384]{1,0:T(8,128)(2,1)} %feat.1, s32[1,128]{1,0:T(1,128)} %bitcast.9, s32[1,16384]{1,0:T(1,128)} %bitcast.5, s32[1,16384]{1,0:T(1,128)} %bitcast.6, s32[1,16384]{1,0:T(1,128)} %bitcast.7), custom_call_target="tpu_custom_call" | custom-call | tf_op jit(solution)/shard_map/similarity/pallas_call | solution.py:282
  106.1 0.8 reduce
  107.0 2.0 %multiply_divide_fusion = f32[32,4096]{1,0:T(8,128)} fusion(f32[32,4096]{1,0:T(8,128)} %get-tuple-element.8, f32[4096]{0:T(1024)} %bitcast.8, f32[32]{0:T(128)S(1)} %reduce), kind=kLoop, calls=%fused_computation | loop fusion | flops 262144 | bytes 1065088 | tf_op jit(solution)/shard_map/div | solution.py:303

commit v2 on v1

v2 whole, which is shorter than its diff:
```python
import functools

import jax
import jax.numpy as jnp
from jax import lax
from jax.experimental import pallas as pl
from jax.experimental.pallas import tpu as pltpu
from jax.sharding import PartitionSpec as P

WIN = 256
PRIME = 65521
AHEAD = 2
MESH = pl.DeviceIdType.MESH


class Plan:
    def __init__(self, rows, tiles, users, columns):
        self.rows, self.tiles, self.users, self.columns = rows, tiles, users, columns
        self.outer, self.inner = 2, tiles // 2
        self.tile_cols = columns // tiles
        self.tile_rows = WIN // rows
        self.width = 128
        units = self.tile_cols // self.width
        self.pieces = max(1, (units - 4) // 4)
        self.sub = self.pieces * self.width
        self.rest = (self.tile_cols - 4 * self.sub) // 2
        self.group = (2 * self.inner, 2 * self.outer)
        self.adds = (self.outer, self.inner)


def fold(h):
    return (h >> 16) * 15 + (h & 65535)


def kernel(
    plan, feat_hbm, salt, mult, offset, thr, out,
    feat, saltc, q0, q1, qt0, qt1, s0, s1, r0, r1, p0, p1, g0, g1, acc, fin,
    zs, zr, zpart, zfin, zsum, zgot, sq, sqr, sqa, sqf,
    feat_sem, q_send, q_recv, a_send0, a_recv0, a_send1, a_recv1, b_send0, b_recv0, b_send1, b_recv1,
    c_send, c_recv, d_send, d_recv, e_send, e_recv, z_send, z_recv, y_send, y_recv, t_send, t_recv,
):
    R, T, users, width, K = plan.rows, plan.tiles, plan.users, plan.width, plan.pieces
    A, B, CT, sub, RB, rest = plan.outer, plan.inner, plan.tile_cols, plan.sub, plan.tile_rows, plan.rest
    chips = (B, A)
    adds = plan.adds
    r, t = lax.axis_index("rows"), lax.axis_index("tiles")
    c = lax.rem(r, 2)
    base = r - c
    partner = (base + 1 - c, t)
    a, b = t // B, lax.rem(t, B)
    q_in, qt, s, rc, part, got = (q0, q1), (qt0, qt1), (s0, s1), (r0, r1), (p0, p1), (g0, g1)
    a_sem, b_sem = ((a_send0, a_recv0), (a_send1, a_recv1)), ((b_send0, b_recv0), (b_send1, b_recv1))

    feat_copy = pltpu.make_async_copy(feat_hbm, feat, feat_sem.at[0])
    feat_copy.start()
    barrier = pltpu.get_barrier_semaphore()
    for d in range(1, 2 * T):
        other = lax.rem(t * 2 + c + d, 2 * T)
        pl.semaphore_signal(
            barrier, inc=1, device_id=(base + lax.rem(other, 2), other // 2), device_id_type=MESH
        )
    for d in range(1, R):
        pl.semaphore_signal(barrier, inc=1, device_id=(lax.rem(r + d, R), t), device_id_type=MESH)

    def along(p, j):
        return lax.rem(b + j, B) if p == 0 else lax.rem(a + j, A)

    def member(p, j, core):
        return (base + core, a * B + along(p, j) if p == 0 else along(p, j) * B + b)

    def core_of(other):
        return 1 - c if other else c

    def adder(p, e):
        if p == 0:
            return (r, lax.rem(a + e, A) * B + b)
        return (r, a * B + lax.rem(b + e, B))

    def remote(src, dst, send, recv, to):
        return pltpu.make_async_remote_copy(
            src_ref=src, dst_ref=dst, send_sem=send, recv_sem=recv, device_id=to, device_id_type=MESH
        )

    def targets(p):
        return [(j, other) for j in range(chips[p]) for other in (0, 1) if j or other]

    def q_copy(p, j, to):
        slot = 2 * j + c
        return lambda src_slot, sem: remote(
            q_in[p].at[src_slot], q_in[p].at[slot], q_send.at[p, sem], q_recv.at[p, slot], to
        )

    def q_direct(p, j):
        return q_copy(p, j, member(p, j, c))(c, 2 * j)

    def q_onchip(p, j):
        return q_copy(p, j, partner)(2 * j + c, 2 * j + 1)

    def q_wait(p, j, core):
        slot = 2 * j + core
        remote(q_in[p].at[slot], q_in[p].at[slot], q_send.at[p, slot], q_recv.at[p, slot], partner).wait_recv()

    def a_copy(p, k, j, other):
        slot = 2 * j + c
        return remote(
            s[p].at[k, 2 * j + other],
            rc[p].at[k, pl.ds(pl.multiple_of(slot * users, users), users)],
            a_sem[p][0].at[k, 2 * j + other], a_sem[p][1].at[k, slot], member(p, j, core_of(other)),
        )

    def a_wait(p, k, j, other):
        slot = 2 * j + core_of(other)
        remote(
            s[p].at[k, 2 * j + other],
            rc[p].at[k, pl.ds(pl.multiple_of(slot * users, users), users)],
            a_sem[p][0].at[k, 2 * j + other], a_sem[p][1].at[k, slot], partner,
        ).wait_recv()

    def b_copy(p, k, e):
        return remote(
            part[p].at[k, e], got[p].at[k, e - 1], b_sem[p][0].at[k, e - 1], b_sem[p][1].at[k, e - 1], adder(p, e)
        )

    def rows_of(other):
        return pl.ds(pl.multiple_of(other * RB, RB), RB)

    def c_copy(p, k, d):
        other = lax.rem(r + d, R)
        return remote(
            acc.at[p, k, rows_of(other)], fin.at[p, k, d - 1],
            c_send.at[p, k, d - 1], c_recv.at[p, k, d - 1], (other, t),
        )

    def d_copy(d):
        other = lax.rem(t + d, T)
        return remote(sq.at[other], sqr.at[d - 1], d_send.at[d - 1], d_recv.at[d - 1], (r, other))

    def e_copy(d):
        return remote(sqa, sqf.at[d - 1], e_send.at[d - 1], e_recv.at[d - 1], (lax.rem(r + d, R), t))

    def z_copy():
        return remote(
            zs, zr.at[pl.ds(pl.multiple_of(c * users, users), users)], z_send.at[0], z_recv.at[0], partner
        )

    def y_copy(d):
        other = lax.rem(r + d, R)
        return remote(
            zpart.at[rows_of(other)], zfin.at[d - 1], y_send.at[d - 1], y_recv.at[d - 1], (other, t)
        )

    def t_copy(d):
        other = lax.rem(t + d, T)
        return remote(zsum.at[other], zgot.at[d - 1], t_send.at[d - 1], t_recv.at[d - 1], (r, other))

    step = min(users, 64)

    def sample(start, size, store):
        cols = pl.ds(pl.multiple_of(start, 128), size)
        by, plus, limit = mult[:, cols], offset[:, cols], thr[:, cols]
        weight = lax.rsqrt(limit.astype(jnp.float32) / float(PRIME))

        def body(i, total):
            rows = pl.ds(pl.multiple_of(i * step, step), step)
            x = feat[rows, cols].astype(jnp.float32)
            h = fold(fold(saltc[rows, :] * by + plus))
            h = jnp.where(h >= PRIME, h - PRIME, h)
            value = x * weight
            store(pl.multiple_of(i * step, step), jnp.where(h < limit, value, jnp.zeros_like(value)))
            return total + jnp.sum((x * x).reshape(step // 8, 8, size), axis=0)

        total = lax.fori_loop(0, users // step, body, jnp.zeros((8, size), jnp.float32))
        return jnp.sum(total, axis=0, keepdims=True)

    def sample_for(p, k, chip, core, store):
        for e in range(adds[p]):
            if p == 0:
                tile = lax.rem(a + e, A) * B + chip
            else:
                tile = chip * B + lax.rem(b + e, B)
            inside = (2 * p + core) * sub + k * width
            squares = sample(tile * CT + inside, width, functools.partial(store, e))
            sq[tile, :, pl.ds(pl.multiple_of(inside, 128), width)] = squares

    def gather_piece(k):
        def keep(p, row0, e, row, value):
            rc[p][k, pl.ds(row0 + row, step), pl.ds(e * width, width)] = value

        def away(p, slot, e, row, value):
            s[p][k, slot, pl.ds(row, step), pl.ds(e * width, width)] = value

        for j, other in sorted(set(targets(0) + targets(1)), key=lambda x: (x[0] == 0, x)):
            for p in range(2):
                if j < chips[p]:
                    sample_for(p, k, along(p, j), core_of(other), functools.partial(away, p, 2 * j + other))
                    a_copy(p, k, j, other).start()
        for p in range(2):
            sample_for(p, k, along(p, 0), c, functools.partial(keep, p, pl.multiple_of(c * users, users)))

    def sample_rest(core, store):
        def tile_body(tile, _):
            inside = 4 * sub + core * rest
            squares = sample(
                tile * CT + inside, rest, functools.partial(store, pl.multiple_of(tile * rest, 128))
            )
            sq[tile, :, pl.ds(pl.multiple_of(inside, 128), rest)] = squares
            return 0

        lax.fori_loop(0, T, tile_body, 0)

    diagonal = lax.broadcasted_iota(jnp.int32, (users, users), 0) == lax.broadcasted_iota(
        jnp.int32, (users, users), 1
    )
    spread = jnp.where(diagonal, jnp.broadcast_to(salt[...].astype(jnp.float32), (users, users)), 0.0)
    saltc[...] = jnp.sum(spread, axis=1, keepdims=True).astype(jnp.int32)

    def store_q(row, value):
        for p in range(2):
            q_in[p][c, pl.ds(row, step), :] = value

    feat_copy.wait()
    q_squares = sample(0, WIN, store_q)
    for tile in range(T):
        sq[tile, :, pl.ds(CT, WIN)] = q_squares
    pl.semaphore_wait(barrier, 2 * T - 1 + R - 1)

    for p in range(2):
        for j in range(1, chips[p]):
            q_direct(p, j).start()
    for p in range(2):
        q_onchip(p, 0).start()
    gather_piece(0)

    def store_zs(col, row, value):
        zs[pl.ds(row, step), pl.ds(col, rest)] = value

    def store_zr(col, row, value):
        zr[pl.ds(pl.multiple_of(c * users, users) + row, step), pl.ds(col, rest)] = value

    def turn(p, slot):
        return q_in[p][slot].T.astype(jnp.bfloat16)

    sample_rest(1 - c, store_zs)
    z_copy().start()
    sample_rest(c, store_zr)
    for k in range(1, min(AHEAD, K)):
        gather_piece(k)
    for p in range(2):
        q_wait(p, 0, 1 - c)
        for slot in range(2):
            qt[p][:, pl.ds(slot * users, users)] = turn(p, slot)
    for p in range(2):
        for j in range(1, chips[p]):
            q_wait(p, j, c)
            q_onchip(p, j).start()
    z_copy().wait_recv()
    for tile in range(T):
        cols = pl.ds(tile * rest, rest)
        zpart[:, cols] = jnp.dot(
            qt[0][:, pl.ds(0, 2 * users)], zr[:, cols].astype(jnp.bfloat16), preferred_element_type=jnp.float32
        )
    for d in range(1, R):
        y_copy(d).start()
    for p in range(2):
        for j in range(1, chips[p]):
            q_wait(p, j, 1 - c)
            for slot in (2 * j, 2 * j + 1):
                qt[p][:, pl.ds(slot * users, users)] = turn(p, slot)

    for k in range(K + 1):
        if k < K:
            for p in range(2):
                for j, other in targets(p):
                    a_wait(p, k, j, other)
                product = jnp.dot(
                    qt[p][...], rc[p][k].astype(jnp.bfloat16), preferred_element_type=jnp.float32
                )
                for e in list(range(1, adds[p])) + [0]:
                    part[p][k, e] = product[:, e * width : (e + 1) * width]
                    if e:
                        b_copy(p, k, e).start()
        if k + AHEAD < K:
            gather_piece(k + AHEAD)
        if k == max(0, K - 1 - AHEAD):
            for d in range(1, T):
                d_copy(d).start()
        if k == K - 1:
            for d in range(1, T):
                t_copy(d).start()
        if k >= 1:
            for p in range(2):
                total = part[p][k - 1, 0]
                for e in range(1, adds[p]):
                    b_copy(p, k - 1, e).wait_recv()
                    total = total + got[p][k - 1, e - 1]
                acc[p, k - 1] = total
                for d in range(1, R):
                    c_copy(p, k - 1, d).start()
        if k == max(0, K - 2):
            same, cross = zpart[rows_of(r)], None
            for d in range(1, R):
                y_copy(d).wait_recv()
                if d % 2 == 0:
                    same = same + zfin[d - 1]
                else:
                    cross = zfin[d - 1] if cross is None else cross + zfin[d - 1]
            for tile in range(T):
                zsum[tile, rows_of(c)] = same[:, tile * rest : (tile + 1) * rest]
                zsum[tile, rows_of(1 - c)] = cross[:, tile * rest : (tile + 1) * rest]
        if k == K - 1:
            total = sq[t]
            for d in range(1, T):
                d_copy(d).wait_recv()
                total = total + sqr[d - 1]
            sqa[...] = total
            for d in range(1, R):
                e_copy(d).start()

    squares = sqa[...]
    for d in range(1, R):
        e_copy(d).wait_recv()
        squares = squares + sqf[d - 1]
    norms = jnp.sqrt(squares + 1e-06)
    sqa_mine = lax.broadcasted_iota(jnp.int32, (RB, WIN), 1) == r * RB + lax.broadcasted_iota(
        jnp.int32, (RB, WIN), 0
    )
    query_norms = jnp.sum(
        jnp.where(sqa_mine, jnp.broadcast_to(norms[:, CT:], (RB, WIN)), 0.0), axis=1, keepdims=True
    )
    sqr[0] = norms

    def put(start, value):
        cols = pl.ds(pl.multiple_of(start, 128), value.shape[1])
        out[:, cols] = value / (query_norms * sqr[0, :, cols])

    total = zsum[t]
    for d in range(1, T):
        t_copy(d).wait_recv()
        total = total + zgot[d - 1]
    for core in range(2):
        put(4 * sub + core * rest, total[core * RB : (core + 1) * RB])

    for k in range(K):
        for p in range(2):
            same, cross = acc[p, k, rows_of(r)], None
            for d in range(1, R):
                c_copy(p, k, d).wait_recv()
                piece = fin[p, k, d - 1]
                if d % 2 == 0:
                    same = same + piece
                else:
                    cross = piece if cross is None else cross + piece
            put((2 * p + c) * sub + k * width, same)
            put((2 * p + 1 - c) * sub + k * width, cross)

    for p in range(2):
        for j in range(chips[p]):
            if j:
                q_direct(p, j).wait_send()
            q_onchip(p, j).wait_send()
    z_copy().wait_send()
    for k in range(K):
        for p in range(2):
            for j, other in targets(p):
                a_copy(p, k, j, other).wait_send()
            for e in range(1, adds[p]):
                b_copy(p, k, e).wait_send()
            for d in range(1, R):
                c_copy(p, k, d).wait_send()
    for d in range(1, T):
        d_copy(d).wait_send()
        t_copy(d).wait_send()
    for d in range(1, R):
        e_copy(d).wait_send()
        y_copy(d).wait_send()


def shards(features, row_salt, column_multiplier, column_offset, thresholds):
    users, columns = features.shape
    plan = Plan(lax.axis_size("rows"), lax.axis_size("tiles"), users, columns)
    R, T, K, width, CT, RB = plan.rows, plan.tiles, plan.pieces, plan.width, plan.tile_cols, plan.tile_rows
    f32, vmem = jnp.float32, pltpu.VMEM
    G, U = plan.group, plan.adds

    def pair(make):
        return [make(0), make(1)]

    def sems(*shape):
        return [pltpu.SemaphoreType.DMA(shape)] * 2

    rest = plan.rest
    scratch = (
        [vmem((users, columns), features.dtype), vmem((users, 1), jnp.int32)]
        + pair(lambda p: vmem((G[p], users, WIN), f32))
        + pair(lambda p: vmem((WIN, G[p] * users), jnp.bfloat16))
        + pair(lambda p: vmem((K, G[p], users, U[p] * width), f32))
        + pair(lambda p: vmem((K, G[p] * users, U[p] * width), f32))
        + pair(lambda p: vmem((K, U[p], WIN, width), f32))
        + pair(lambda p: vmem((K, U[p] - 1, WIN, width), f32))
        + [vmem((2, K, WIN, width), f32), vmem((2, K, R - 1, RB, width), f32)]
        + [vmem((users, T * rest), f32), vmem((2 * users, T * rest), f32), vmem((WIN, T * rest), f32)]
        + [vmem((R - 1, RB, T * rest), f32), vmem((T, 2 * RB, rest), f32), vmem((T - 1, 2 * RB, rest), f32)]
        + [vmem((T, 1, CT + WIN), f32), vmem((T - 1, 1, CT + WIN), f32)]
        + [vmem((1, CT + WIN), f32), vmem((R - 1, 1, CT + WIN), f32)]
        + [pltpu.SemaphoreType.DMA((1,))]
        + sems(2, max(G))
        + sems(K, G[0]) + sems(K, G[1])
        + sems(K, U[0] - 1) + sems(K, U[1] - 1)
        + sems(2, K, R - 1) + sems(T - 1) + sems(R - 1)
        + sems(1) + sems(R - 1) + sems(T - 1)
    )
    spec = pl.BlockSpec(memory_space=pltpu.VMEM)
    return pl.pallas_call(
        functools.partial(kernel, plan),
        out_shape=jax.ShapeDtypeStruct((RB, CT), f32),
        in_specs=[pl.BlockSpec(memory_space=pl.ANY)] + [spec] * 4,
        out_specs=spec,
        scratch_shapes=scratch,
        compiler_params=pltpu.CompilerParams(
            collective_id=0, has_side_effects=True, vmem_limit_bytes=60 * 1024 * 1024
        ),
        name="similarity",
    )(
        features,
        row_salt.reshape(1, users),
        column_multiplier.reshape(1, columns),
        column_offset.reshape(1, columns),
        thresholds.reshape(1, columns),
    )


def solution(mesh):
    placed = (P(("rows", "tiles"), None), P(("rows", "tiles")), P(), P(), P())
    return jax.shard_map(
        shards, mesh=mesh, in_specs=placed, out_specs=P("rows", "tiles"), check_vma=False
    )
```

time: 109 us -> 89.9 us (0.82)
  Pallas kernels: 106 us -> 87.8 us
  other arithmetic: 2.82 us -> 0 us
  local copies, waits for them, and re-layouts: 0 us -> 1.87 us
    pallas_call x1, Pallas kernels: 106 us -> 87.8 us  [shards(): pl.pallas_call(functools.partial(kernel, plan), out_shape=jax.ShapeDtypeS...]
    div x1 -> x0, other arithmetic: 1.98 us -> none  [shards(): return gram / (query_norms * column_norms)]
    unnamed x0 -> x1, local copies, waits for them, and re-layouts: none -> 1.87 us
where the time goes in v2:
time: 89.9 us; the launch traced here: 89.7 us
  Pallas kernels  87.8 us (98%)
  local copies, waits for them, and re-layouts  1.87 us (2%)
    pallas_call x1, Pallas kernels, shards(): pl.pallas_call(functools.partial(kernel, plan), out_shape=jax.ShapeDtypeS...  87.8 us
    unnamed x1, local copies, waits for them, and re-layouts  1.87 us

profile of v2, /device:TPU:0, one launch (start us, length us, event | category | flops | bytes accessed | tf_op | source)
XLA Modules:
  0.0 89.7 jit_solution(11899579708206374637)
XLA Ops:
  0.0 87.8 %similarity.1 = f32[32,4096]{1,0:T(8,128)} custom-call(bf16[128,16384]{1,0:T(8,128)(2,1)} %feat_hbm.1, s32[1,128]{1,0:T(1,128)} %bitcast.7, s32[1,16384]{1,0:T(1,128)} %bitcast.4, s32[1,16384]{1,0:T(1,128)} %bitcast.5, s32[1,16384]{1,0:T(1,128)} %bitcast.6), custom_call_target="tpu_custom_call" | custom-call | tf_op jit(solution)/shard_map/similarity/pallas_call | solution.py:413
  87.8 1.9 %copy.7 = f32[32,4096]{1,0:T(8,128)} copy(f32[32,4096]{1,0:T(8,128)} %similarity.1) | data formatting | bytes 1048576

commit v3 on v2

--- a/solution.py
+++ b/solution.py
@@ -307,7 +307,7 @@
             for tile in range(T):
                 zsum[tile, rows_of(c)] = same[:, tile * rest : (tile + 1) * rest]
                 zsum[tile, rows_of(1 - c)] = cross[:, tile * rest : (tile + 1) * rest]
-        if k == K - 1:
+        if k == max(0, K - 2):
             total = sq[t]
             for d in range(1, T):
                 d_copy(d).wait_recv()

time: 89.9 us -> 88.5 us (0.984)
  Pallas kernels: 87.8 us -> 86.3 us
    pallas_call x1, Pallas kernels: 87.8 us -> 86.3 us  [shards(): pl.pallas_call(functools.partial(kernel, plan), out_shape=jax.ShapeDtypeS...]
where the time goes in v3:
time: 88.5 us; the launch traced here: 88.2 us
  Pallas kernels  86.3 us (98%)
  local copies, waits for them, and re-layouts  1.87 us (2%)
    pallas_call x1, Pallas kernels, shards(): pl.pallas_call(functools.partial(kernel, plan), out_shape=jax.ShapeDtypeS...  86.3 us
    unnamed x1, local copies, waits for them, and re-layouts  1.87 us

profile of v3, /device:TPU:0, one launch (start us, length us, event | category | flops | bytes accessed | tf_op | source)
XLA Modules:
  0.0 88.2 jit_solution(8482131738435029617)
XLA Ops:
  0.0 86.3 %similarity.1 = f32[32,4096]{1,0:T(8,128)} custom-call(bf16[128,16384]{1,0:T(8,128)(2,1)} %feat_hbm.1, s32[1,128]{1,0:T(1,128)} %bitcast.7, s32[1,16384]{1,0:T(1,128)} %bitcast.4, s32[1,16384]{1,0:T(1,128)} %bitcast.5, s32[1,16384]{1,0:T(1,128)} %bitcast.6), custom_call_target="tpu_custom_call" | custom-call | tf_op jit(solution)/shard_map/similarity/pallas_call | solution.py:413
  86.4 1.9 %copy.7 = f32[32,4096]{1,0:T(8,128)} copy(f32[32,4096]{1,0:T(8,128)} %similarity.1) | data formatting | bytes 1048576
